TPU v7x, 512 devices: a whole 4x4x16 slice. The times are simulated.
512 devices in a mesh: kz: 16 (over x, y_hi, core), en: 32 (over y_lo, z).
Axes of the slice: x: 4, y: 4 (y_hi: 2, y_lo: 2; y = y_hi * 2 + y_lo), z: 16, core: 2. Of those that a mesh axis runs over, the one named last changes fastest.
Arguments:
- green: bfloat16 [32, 2, 144, 4096], P('kz', None, None, 'en'), may hold values from -6 to 6
- coupling: bfloat16 [32, 82944], replicated, may hold values from -0.03125 to 0.03125
- kdiff: int32 [32, 32], replicated, may hold values from 0 to 31, each once within a row
- shift: int32 [32], replicated, may hold values from 1 to 8, as said below
- emit_weight: float32 [32], replicated, may hold values from 0.3 to 3
- absorb_weight: float32 [32], replicated, may hold values from 0.3 to 3
- neighbours: int32 [16, 4], replicated, may hold values from 0 to 15
Outputs:
- sigma: float32 [32, 2, 144, 4096], P('kz', None, None, 'en')
Inputs may be any that keep to these rules, and one draw needn't show every extreme that they name: `kdiff`: every row names each momentum point once. `shift`: some entry equals 8.
All inputs are finite; a program needn't handle non-finite values.
Results may differ from a plain program's by a relative error of at most 0.0029.
Values may be sent and summed in bfloat16 or wider, within the bound.
A program may use at most 128 MiB of HBM per device.

v0:
```python
import jax
import jax.numpy as jnp
from jax import lax
from jax.sharding import PartitionSpec as P

HALO = 8


def extended(value, sides, width):
    for axis, dim in sides:
        peers, length = (lax.axis_size(axis), value.shape[dim])
        up = [(i, (i + 1) % peers) for i in range(peers - 1)]
        down = [(j, i) for i, j in up]
        last = lax.slice_in_dim(value, length - width, length, axis=dim)
        first = lax.slice_in_dim(value, 0, width, axis=dim)
        before = lax.ppermute(last, axis, up)
        after = lax.ppermute(first, axis, down)
        value = jnp.concatenate([before, value, after], axis=dim)
    return value


def on_device(green, coupling, kdiff, shift, emit_weight, absorb_weight, neighbours):
    atoms = neighbours.shape[0]
    cols = green.shape[3]
    blocks = green.shape[2]
    local_points = green.shape[0]
    energies = cols // atoms
    margin = HALO * atoms
    whole = lax.all_gather(green, "kz", axis=0, tiled=True)
    widened = extended(whole, (("en", 3),), margin)
    all_points = kdiff.shape[0]
    krows = lax.dynamic_slice_in_dim(kdiff, lax.axis_index("kz") * local_points, local_points, 0)
    couple_all = coupling.reshape(all_points, 4, blocks, blocks)
    phonons = jnp.arange(all_points, dtype=jnp.int32)

    def select_mix(phonon, source_point):
        steps_off = shift[phonon]
        block = lax.dynamic_index_in_dim(widened, source_point, 0, keepdims=False)
        early = lax.dynamic_slice_in_dim(block, (HALO - steps_off) * atoms, cols, 2)
        late = lax.dynamic_slice_in_dim(block, (HALO + steps_off) * atoms, cols, 2)
        mixed = emit_weight[phonon] * early.astype(jnp.float32) + absorb_weight[
            phonon
        ] * late.astype(jnp.float32)
        return mixed.astype(jnp.bfloat16)

    results = []
    for local in range(local_points):
        mixes = jax.vmap(select_mix)(phonons, krows[local])
        projected = jnp.einsum(
            "qjmn,qrnc->jrmc", couple_all, mixes, preferred_element_type=jnp.float32
        )
        projected = projected.reshape(4, 2, blocks, energies, atoms)
        total = jnp.take(projected[0], neighbours[:, 0], axis=3)
        for slot in range(1, 4):
            total = total + jnp.take(projected[slot], neighbours[:, slot], axis=3)
        results.append(total.reshape(2, blocks, cols))
    return jnp.stack(results, 0)


def solution(mesh):
    return jax.shard_map(
        on_device,
        mesh=mesh,
        in_specs=(P("kz", None, None, "en"), P(), P(), P(), P(), P(), P()),
        out_specs=P("kz", None, None, "en"),
        check_vma=False,
    )
```

profile of v0, /device:TPU:8, one launch (start us, length us, event | category | flops | bytes accessed | tf_op | source)
XLA Modules:
  0.0 365.7 jit_solution(10156546521841482820)
XLA Ops:
  6.5 0.0 copy-start
  6.5 0.0 all-gather.2.cloned.1.call-start
  6.5 0.7 all-gather.2.cloned.1.call-update
  7.3 71.4 %all-gather.2.cloned.1.call-done = bf16[32,2,144,128]{3,2,1,0:T(8,128)(2,1)} async-done(((bf16[2,2,144,128]{3,2,1,0:T(8,128)(2,1)}), bf16[32,2,144,128]{3,2,1,0:T(8,128)(2,1)}) %all-gather.2.cloned.1.call-update) | async-done | bytes 2359312 | tf_op jit(solution)/shard_map/all_gather | solution.py:29
  78.6 3.5 collective-permute-start
  82.1 5.3 %collective-permute-start.1 = (bf16[32,2,144,128]{3,2,1,0:T(8,128)(2,1)}, bf16[32,2,144,128]{3,2,1,0:T(8,128)(2,1)}, u32[]{:S(2)}, u32[]{:S(2)}) collective-permute-start(bf16[32,2,144,128]{3,2,1,0:T(8,128)(2,1)} %all-gather.2.cloned.1.call-done), channel_id=1, source_target_pairs={{1,0},{2,1},{3,2},{4,3},{5,4},{6,5},{7,6},{8,7},{9,8},{10,9},{11,1... | collective-permute-start | bytes 7077896 | tf_op jit(solution)/shard_map/ppermute | solution.py:17
  87.4 1.4 gather_fusion.2
  88.8 1.4 gather_fusion.3
  90.1 1.4 gather_fusion
  91.5 18.6 %reshape.120 = bf16[32,4,144,144]{3,2,1,0:T(8,128)(2,1)} reshape(bf16[32,82944]{1,0:T(8,128)(2,1)} %param.10) | data formatting | bytes 10616832 | tf_op jit(solution)/shard_map/reshape | solution.py:33
  110.1 0.0 copy-start.2
  110.1 0.0 copy-done
  110.1 0.0 copy-done.3
  110.2 27.2 %collective-permute-done = bf16[32,2,144,128]{3,2,1,0:T(8,128)(2,1)} collective-permute-done((bf16[32,2,144,128]{3,2,1,0:T(8,128)(2,1)}, bf16[32,2,144,128]{3,2,1,0:T(8,128)(2,1)}, u32[]{:S(2)}, u32[]{:S(2)}) %collective-permute-start) | collective-permute-done | bytes 2359328 | tf_op jit(solution)/shard_map/ppermute | solution.py:16
  137.4 3.4 constant_dynamic-update-slice_fusion.2
  140.8 0.0 copy-done.2
  140.8 1.6 constant_dynamic-update-slice_fusion.1
  142.4 0.0 collective-permute-done.1
  142.4 3.4 constant_dynamic-update-slice_fusion
  145.8 7.5 %gather_fusion.1 = bf16[32,2,144,384]{3,2,1,0:T(8,128)(2,1)} fusion(bf16[32,2,144,384]{3,2,1,0:T(8,128)(2,1)} %constant_dynamic-update-slice_fusion, s32[32]{0:T(128)S(1)} %get-tuple-element.32), kind=kCustom, calls=%fused_computation.9 | custom fusion | bytes 14156288 | tf_op jit(solution)/shard_map/vmap(jit(dynamic_index_in_dim))/gather | solution.py:38
  153.3 30.6 %copy.70 = bf16[32,2,144,384]{2,1,0,3:T(2,128)(2,1)} copy(bf16[32,2,144,384]{3,2,1,0:T(8,128)(2,1)} %gather_fusion.1) | data formatting | bytes 14155776 | tf_op jit(solution)/shard_map/vmap(jit(dynamic_index_in_dim))/gather | solution.py:38
  183.9 17.0 %gather_fusion.5 = bf16[32,2,144,128]{2,1,3,0:T(2,128)(2,1)} fusion(bf16[32,2,144,384]{2,1,0,3:T(2,128)(2,1)} %copy.70, s32[32]{0:T(128)S(1)} %get-tuple-element.34), kind=kCustom, calls=%fused_computation.13 | custom fusion | bytes 4719104 | tf_op jit(solution)/shard_map/vmap()/gather | solution.py:39
  200.9 17.0 %gather_fusion.6 = bf16[32,2,144,128]{2,1,3,0:T(2,128)(2,1)} fusion(bf16[32,2,144,384]{2,1,0,3:T(2,128)(2,1)} %copy.70, s32[32]{0:T(128)S(1)} %get-tuple-element.35), kind=kCustom, calls=%fused_computation.14 | custom fusion | bytes 4719104 | tf_op jit(solution)/shard_map/vmap()/gather | solution.py:40
  217.9 7.5 %gather_fusion.4 = bf16[32,2,144,384]{3,2,1,0:T(8,128)(2,1)} fusion(bf16[32,2,144,384]{3,2,1,0:T(8,128)(2,1)} %constant_dynamic-update-slice_fusion, s32[32]{0:T(128)S(1)} %get-tuple-element.33), kind=kCustom, calls=%fused_computation.12 | custom fusion | bytes 14156288 | tf_op jit(solution)/shard_map/vmap(jit(dynamic_index_in_dim))/gather | solution.py:38
  225.3 30.6 %copy.85 = bf16[32,2,144,384]{2,1,0,3:T(2,128)(2,1)} copy(bf16[32,2,144,384]{3,2,1,0:T(8,128)(2,1)} %gather_fusion.4) | data formatting | bytes 14155776 | tf_op jit(solution)/shard_map/vmap(jit(dynamic_index_in_dim))/gather | solution.py:38
  255.9 17.0 %gather_fusion.7 = bf16[32,2,144,128]{2,1,3,0:T(2,128)(2,1)} fusion(bf16[32,2,144,384]{2,1,0,3:T(2,128)(2,1)} %copy.85, s32[32]{0:T(128)S(1)} %get-tuple-element.34), kind=kCustom, calls=%fused_computation.15 | custom fusion | bytes 4719104 | tf_op jit(solution)/shard_map/vmap()/gather | solution.py:39
  272.9 17.0 %gather_fusion.8 = bf16[32,2,144,128]{2,1,3,0:T(2,128)(2,1)} fusion(bf16[32,2,144,384]{2,1,0,3:T(2,128)(2,1)} %copy.85, s32[32]{0:T(128)S(1)} %get-tuple-element.35), kind=kCustom, calls=%fused_computation.16 | custom fusion | bytes 4719104 | tf_op jit(solution)/shard_map/vmap()/gather | solution.py:40
  290.0 9.3 %copy.71 = bf16[32,2,144,128]{3,2,1,0:T(8,128)(2,1)S(1)} copy(bf16[32,2,144,128]{2,1,3,0:T(2,128)(2,1)} %gather_fusion.5) | data formatting | bytes 4718592 | tf_op jit(solution)/shard_map/vmap()/gather | solution.py:39
  299.3 10.6 %copy.73 = bf16[32,2,144,128]{3,2,1,0:T(8,128)(2,1)} copy(bf16[32,2,144,128]{2,1,3,0:T(2,128)(2,1)} %gather_fusion.6) | data formatting | bytes 4718592 | tf_op jit(solution)/shard_map/vmap()/gather | solution.py:40
  309.9 10.7 %copy.86 = bf16[32,2,144,128]{3,2,1,0:T(8,128)(2,1)} copy(bf16[32,2,144,128]{2,1,3,0:T(2,128)(2,1)} %gather_fusion.7) | data formatting | bytes 4718592 | tf_op jit(solution)/shard_map/vmap()/gather | solution.py:39
  320.6 10.6 %copy.88 = bf16[32,2,144,128]{3,2,1,0:T(8,128)(2,1)} copy(bf16[32,2,144,128]{2,1,3,0:T(2,128)(2,1)} %gather_fusion.8) | data formatting | bytes 4718592 | tf_op jit(solution)/shard_map/vmap()/gather | solution.py:40
  331.2 6.6 %fusion.6 = (bf16[32,2,144,128,1]{3,2,1,0,4:T(8,128)(2,1)}, bf16[32,2,144,128,1]{3,2,1,0,4:T(8,128)(2,1)S(1)}) fusion(bf16[32,2,144,128]{3,2,1,0:T(8,128)(2,1)} %copy.73, bf16[32,2,144,128]{3,2,1,0:T(8,128)(2,1)S(1)} %copy.71, f32[32]{0:T(128)S(1)} %gather_fusion.3, f32[32]{0:T(128)S(1)} %gather_fusion, bf16[32,2,144,128]{3,2,1,0:T(8,128)(2,1)} %copy.88, ...), kind=kLoop, calls=%fused_computation.25 | loop fusion | flops 14155776 | bytes 14156032 | tf_op jit(solution)/shard_map/vmap()/convert_element_type | solution.py:44
  337.8 6.0 %fusion.15 = f32[4,2,144,128]{3,2,0,1:T(8,128)S(1)} fusion(bf16[32,4,144,144]{3,2,1,0:T(8,128)(2,1)} %reshape.120, bf16[32,2,144,128,1]{3,2,1,0,4:T(8,128)(2,1)S(1)} %get-tuple-element.31), kind=kOutput, calls=%fused_computation.30 | convolution fusion | flops 1358954496 | bytes 8257536 | tf_op jit(solution)/shard_map/qjmn,qrnc->jrmc/dot_general | solution.py:49
  343.9 0.1 copy.91
  344.0 0.2 copy.92
  344.2 0.1 copy.93
  344.3 0.2 copy.94
  344.5 0.1 copy.95
  344.6 0.2 copy.96
  344.8 0.1 copy.97
  344.9 0.2 copy.98
  345.1 6.4 %fusion.10 = f32[4,2,144,128]{3,2,0,1:T(8,128)S(1)} fusion(bf16[32,4,144,144]{3,2,1,0:T(8,128)(2,1)} %reshape.120, bf16[32,2,144,128,1]{3,2,1,0,4:T(8,128)(2,1)} %get-tuple-element.30), kind=kOutput, calls=%fused_computation.29 | convolution fusion | flops 1358954496 | bytes 8257536 | tf_op jit(solution)/shard_map/qjmn,qrnc->jrmc/dot_general | solution.py:49
  351.5 0.1 copy.76
  351.7 0.2 copy.77
  351.8 0.6 gather_fusion.13
  352.4 0.6 gather_fusion.9
  353.0 0.1 copy.78
  353.1 0.2 copy.79
  353.3 0.6 gather_fusion.14
  353.8 0.6 gather_fusion.10
  354.4 0.1 copy.80
  354.5 0.2 copy.81
  354.7 0.6 gather_fusion.15
  355.3 0.6 gather_fusion.11
  355.8 0.1 copy.82
  356.0 0.2 copy.83
  356.1 0.0 copy-start.1
  356.2 0.6 gather_fusion.16
  356.7 0.6 gather_fusion.12
  357.3 0.2 bitcast_add_fusion.3
  357.5 0.2 copy.84
  357.7 0.2 copy.99
  357.9 0.9 copy.100
  358.8 0.0 copy-done.1
  (12 shorter events, 0.2 us)
Async XLA Ops:
  6.5 103.5 %copy-start = (s32[32,32]{1,0:T(8,128)S(1)}, s32[32,32]{1,0:T(8,128)}, u32[]{:S(2)}) copy-start(s32[32,32]{1,0:T(8,128)} %param.11) | copy-start | bytes 12292
  6.5 72.1 %all-gather.2.cloned.1.call-start = ((), (), s32[]{:S(2)}) async-start(), calls=%async_computation | async-start | bytes 2506752 | tf_op jit(solution)/shard_map/all_gather | solution.py:29
  78.6 58.8 %collective-permute-start = (bf16[32,2,144,128]{3,2,1,0:T(8,128)(2,1)}, bf16[32,2,144,128]{3,2,1,0:T(8,128)(2,1)}, u32[]{:S(2)}, u32[]{:S(2)}) collective-permute-start(bf16[32,2,144,128]{3,2,1,0:T(8,128)(2,1)} %all-gather.2.cloned.1.call-done), channel_id=1, source_target_pairs={{0,1},{1,2},{2,3},{3,4},{4,5},{5,6},{6,7},{7,8},{8,9},{9,10},{10,1... | collective-permute-start | bytes 7077896 | tf_op jit(solution)/shard_map/ppermute | solution.py:16
  82.1 60.3 %collective-permute-start.1 = (bf16[32,2,144,128]{3,2,1,0:T(8,128)(2,1)}, bf16[32,2,144,128]{3,2,1,0:T(8,128)(2,1)}, u32[]{:S(2)}, u32[]{:S(2)}) collective-permute-start(bf16[32,2,144,128]{3,2,1,0:T(8,128)(2,1)} %all-gather.2.cloned.1.call-done), channel_id=1, source_target_pairs={{1,0},{2,1},{3,2},{4,3},{5,4},{6,5},{7,6},{8,7},{9,8},{10,9},{11,1... | collective-permute-start | bytes 7077896 | tf_op jit(solution)/shard_map/ppermute | solution.py:17
  91.5 18.6 %copy-start.3 = (s32[16,4]{0,1:T(4,128)S(1)}, s32[16,4]{0,1:T(4,128)}, u32[]{:S(2)}) copy-start(s32[16,4]{0,1:T(4,128)} %param.15) | copy-start | bytes 772
  110.1 30.7 %copy-start.2 = (bf16[32,2,144,128]{3,2,1,0:T(8,128)(2,1)S(1)}, bf16[32,2,144,128]{3,2,1,0:T(8,128)(2,1)}, u32[]{:S(2)}) copy-start(bf16[32,2,144,128]{3,2,1,0:T(8,128)(2,1)} %all-gather.2.cloned.1.call-done) | copy-start | bytes 7077892
  356.1 2.7 copy-start.1
Sparse Core Ops, SparseCore 0:
  10.6 67.9 all-gather.1
where the time goes:
time: 369 us; the launch traced here: 366 us
  local copies, waits for them, and re-layouts  225 us (61%)
  waiting for transfers between devices  99.3 us (27%)
  between operations  13.7 us (4%)
  matrix products  12.4 us (3%)
  starting transfers between devices  8.74 us (2%)
  other arithmetic  6.9 us (2%)
    gather x4, local copies, waits for them, and re-layouts, select_mix(): block = lax.dynamic_index_in_dim(widened, source_point, 0, keepdims=False)  76.1 us
    all_gather x1, waiting for transfers between devices, on_device(): whole = lax.all_gather(green, 'kz', axis=0, tiled=True)  71.4 us
    gather x4, local copies, waits for them, and re-layouts, select_mix(): late = lax.dynamic_slice_in_dim(block, (HALO + steps_off) * atoms, cols, 2)  55.3 us
    gather x4, local copies, waits for them, and re-layouts, select_mix(): early = lax.dynamic_slice_in_dim(block, (HALO - steps_off) * atoms, cols, 2)  53.9 us
    ppermute x1, waiting for transfers between devices, extended(): before = lax.ppermute(last, axis, up)  27.2 us
    reshape x1, local copies, waits for them, and re-layouts, on_device(): couple_all = coupling.reshape(all_points, 4, blocks, blocks)  18.6 us
    dot_general x2, matrix products, on_device(): jnp.einsum('qjmn,qrnc->jrmc', couple_all, mixes, preferred_element_type=j...  12.4 us
  transfers between devices with their start and end apart: 3, of which 2 were waited for; matrix products, arithmetic and copies ran while one was open for 8% of the time, Pallas kernels for 0%

commit v1 on v0

--- a/solution.py
+++ b/solution.py
@@ -26,7 +26,9 @@
     local_points = green.shape[0]
     energies = cols // atoms
     margin = HALO * atoms
-    whole = lax.all_gather(green, "kz", axis=0, tiled=True)
+    whole = jnp.concatenate(
+        lax.all_to_all(jnp.stack([green] * lax.axis_size("kz")), "kz", 0, 0), axis=0
+    )
     widened = extended(whole, (("en", 3),), margin)
     all_points = kdiff.shape[0]
     krows = lax.dynamic_slice_in_dim(kdiff, lax.axis_index("kz") * local_points, local_points, 0)

time: 369 us -> 326 us (0.88)
  waiting for transfers between devices: 99.3 us -> 29.9 us
  blocking collectives: 0 us -> 37.6 us
  between operations: 13.7 us -> 0.38 us
  local copies, waits for them, and re-layouts: 225 us -> 216 us
  other arithmetic: 6.9 us -> 12.8 us
  starting transfers between devices: 8.74 us -> 14.1 us
    all_gather x1 -> x0, waiting for transfers between devices: 71.4 us -> none  [on_device(): whole = lax.all_gather(green, 'kz', axis=0, tiled=True)]
    all_to_all x0 -> x1, blocking collectives: none -> 37.6 us  [on_device(): lax.all_to_all(jnp.stack([green] * lax.axis_size('kz')), 'kz', 0, 0)]
    concatenate x0 -> x1, other arithmetic: none -> 5.89 us  [extended(): value = jnp.concatenate([before, value, after], axis=dim)]
    ppermute x1, starting transfers between devices: 5.29 us -> 10.3 us  [extended(): after = lax.ppermute(first, axis, down)]
    unnamed x10 -> x12, local copies, waits for them, and re-layouts: 5.01 us -> 0.03 us
  transfers between devices with their start and end apart: 3 -> 2, of which waited for: 2 -> 2; matrix products, arithmetic and copies ran while one was open for 8% -> 6% of each run, Pallas kernels for 0% -> 0%
where the time goes in v1:
time: 326 us; the launch traced here: 323 us
  local copies, waits for them, and re-layouts  216 us (66%)
  blocking collectives  37.6 us (12%)
  waiting for transfers between devices  29.9 us (9%)
  starting transfers between devices  14.1 us (4%)
  other arithmetic  12.8 us (4%)
  matrix products  12.4 us (4%)
    gather x4, local copies, waits for them, and re-layouts, select_mix(): block = lax.dynamic_index_in_dim(widened, source_point, 0, keepdims=False)  76.1 us
    gather x4, local copies, waits for them, and re-layouts, select_mix(): late = lax.dynamic_slice_in_dim(block, (HALO + steps_off) * atoms, cols, 2)  55.3 us
    gather x4, local copies, waits for them, and re-layouts, select_mix(): early = lax.dynamic_slice_in_dim(block, (HALO - steps_off) * atoms, cols, 2)  54.1 us
    all_to_all x1, blocking collectives, on_device(): lax.all_to_all(jnp.stack([green] * lax.axis_size('kz')), 'kz', 0, 0)  37.6 us
    ppermute x1, waiting for transfers between devices, extended(): before = lax.ppermute(last, axis, up)  28.8 us
    reshape x1, local copies, waits for them, and re-layouts, on_device(): couple_all = coupling.reshape(all_points, 4, blocks, blocks)  18.6 us
    dot_general x2, matrix products, on_device(): jnp.einsum('qjmn,qrnc->jrmc', couple_all, mixes, preferred_element_type=j...  12.4 us
    ppermute x1, starting transfers between devices, extended(): after = lax.ppermute(first, axis, down)  10.3 us
  transfers between devices with their start and end apart: 2, of which 2 were waited for; matrix products, arithmetic and copies ran while one was open for 6% of the time, Pallas kernels for 0%

profile of v1, /device:TPU:8, one launch (start us, length us, event | category | flops | bytes accessed | tf_op | source)
XLA Modules:
  0.0 322.9 jit_solution(13322411211470467201)
XLA Ops:
  0.0 0.0 copy-start
  0.0 0.0 copy-start.2
  0.0 0.0 copy-start.4
  0.0 1.4 stack.4
  1.4 37.6 %all_to_all.5 = bf16[16,2,2,144,128]{4,3,2,1,0:T(8,128)(2,1)S(1)} all-to-all(bf16[16,2,2,144,128]{4,3,2,1,0:T(8,128)(2,1)S(1)} %stack.4), channel_id=1, replica_groups=mesh['kz'=16,'en'=32] {'kz'}, dimensions={0} | all-to-all | bytes 4718592 | tf_op jit(solution)/shard_map/all_to_all | solution.py:30
  39.0 3.8 %collective-permute-start = (bf16[32,2,144,128]{3,2,1,0:T(8,128)(2,1)S(1)}, bf16[32,2,144,128]{3,2,1,0:T(8,128)(2,1)}, u32[]{:S(2)}, u32[]{:S(2)}) collective-permute-start(bf16[32,2,144,128]{3,2,1,0:T(8,128)(2,1)S(1)} %bitcast.91), channel_id=1, source_target_pairs={{0,1},{1,2},{2,3},{3,4},{4,5},{5,6},{6,7},{7,8},{8,9},{9,10},{10,1... | collective-permute-start | bytes 7077896 | tf_op jit(solution)/shard_map/ppermute | solution.py:16
  42.8 10.3 %collective-permute-start.1 = (bf16[32,2,144,128]{3,2,1,0:T(8,128)(2,1)S(1)}, bf16[32,2,144,128]{3,2,1,0:T(8,128)(2,1)}, u32[]{:S(2)}, u32[]{:S(2)}) collective-permute-start(bf16[32,2,144,128]{3,2,1,0:T(8,128)(2,1)S(1)} %bitcast.92), channel_id=1, source_target_pairs={{1,0},{2,1},{3,2},{4,3},{5,4},{6,5},{7,6},{8,7},{9,8},{10,9},{11,1... | collective-permute-start | bytes 7077896 | tf_op jit(solution)/shard_map/ppermute | solution.py:17
  53.1 0.0 copy-done.2
  53.2 0.7 gather_fusion.2
  53.9 0.0 copy-done.3
  53.9 0.7 gather_fusion.3
  54.6 0.0 copy-done.4
  54.6 0.7 gather_fusion
  55.3 18.6 %reshape.126 = bf16[32,4,144,144]{3,2,1,0:T(8,128)(2,1)} reshape(bf16[32,82944]{1,0:T(8,128)(2,1)} %param.10) | data formatting | bytes 10616832 | tf_op jit(solution)/shard_map/reshape | solution.py:35
  73.9 0.0 copy-done
  73.9 0.0 copy-done.5
  74.0 28.8 %collective-permute-done = bf16[32,2,144,128]{3,2,1,0:T(8,128)(2,1)} collective-permute-done((bf16[32,2,144,128]{3,2,1,0:T(8,128)(2,1)S(1)}, bf16[32,2,144,128]{3,2,1,0:T(8,128)(2,1)}, u32[]{:S(2)}, u32[]{:S(2)}) %collective-permute-start) | collective-permute-done | bytes 2359328 | tf_op jit(solution)/shard_map/ppermute | solution.py:16
  102.8 1.1 collective-permute-done.1
  103.9 5.9 %pad_maximum_fusion = bf16[32,2,144,384]{3,2,1,0:T(8,128)(2,1)} fusion(bf16[32,2,144,128]{3,2,1,0:T(8,128)(2,1)} %collective-permute-done.1, bf16[32,2,144,128]{3,2,1,0:T(8,128)(2,1)S(1)} %bitcast.93, bf16[32,2,144,128]{3,2,1,0:T(8,128)(2,1)} %collective-permute-done), kind=kLoop, calls=%fused_computation.23 | loop fusion | flops 21233664 | bytes 14155776 | tf_op jit(solution)/shard_map/concatenate | solution.py:18
  109.8 7.5 %gather_fusion.1 = bf16[32,2,144,384]{3,2,1,0:T(8,128)(2,1)} fusion(bf16[32,2,144,384]{3,2,1,0:T(8,128)(2,1)} %pad_maximum_fusion, s32[32]{0:T(128)S(1)} %get-tuple-element.32), kind=kCustom, calls=%fused_computation.9 | custom fusion | bytes 14156288 | tf_op jit(solution)/shard_map/vmap(jit(dynamic_index_in_dim))/gather | solution.py:40
  117.2 30.6 %copy.43 = bf16[32,2,144,384]{2,1,0,3:T(2,128)(2,1)} copy(bf16[32,2,144,384]{3,2,1,0:T(8,128)(2,1)} %gather_fusion.1) | data formatting | bytes 14155776 | tf_op jit(solution)/shard_map/vmap(jit(dynamic_index_in_dim))/gather | solution.py:40
  147.8 16.9 %gather_fusion.5 = bf16[32,2,144,128]{2,1,3,0:T(2,128)(2,1)} fusion(bf16[32,2,144,384]{2,1,0,3:T(2,128)(2,1)} %copy.43, s32[32]{0:T(128)S(1)} %get-tuple-element.34), kind=kCustom, calls=%fused_computation.13 | custom fusion | bytes 4719104 | tf_op jit(solution)/shard_map/vmap()/gather | solution.py:41
  164.8 17.0 %gather_fusion.6 = bf16[32,2,144,128]{2,1,3,0:T(2,128)(2,1)} fusion(bf16[32,2,144,384]{2,1,0,3:T(2,128)(2,1)} %copy.43, s32[32]{0:T(128)S(1)} %get-tuple-element.35), kind=kCustom, calls=%fused_computation.14 | custom fusion | bytes 4719104 | tf_op jit(solution)/shard_map/vmap()/gather | solution.py:42
  181.8 7.5 %gather_fusion.4 = bf16[32,2,144,384]{3,2,1,0:T(8,128)(2,1)} fusion(bf16[32,2,144,384]{3,2,1,0:T(8,128)(2,1)} %pad_maximum_fusion, s32[32]{0:T(128)S(1)} %get-tuple-element.33), kind=kCustom, calls=%fused_computation.12 | custom fusion | bytes 14156288 | tf_op jit(solution)/shard_map/vmap(jit(dynamic_index_in_dim))/gather | solution.py:40
  189.2 30.6 %copy.58 = bf16[32,2,144,384]{2,1,0,3:T(2,128)(2,1)} copy(bf16[32,2,144,384]{3,2,1,0:T(8,128)(2,1)} %gather_fusion.4) | data formatting | bytes 14155776 | tf_op jit(solution)/shard_map/vmap(jit(dynamic_index_in_dim))/gather | solution.py:40
  219.8 17.2 %gather_fusion.7 = bf16[32,2,144,128]{2,1,3,0:T(2,128)(2,1)} fusion(bf16[32,2,144,384]{2,1,0,3:T(2,128)(2,1)} %copy.58, s32[32]{0:T(128)S(1)} %get-tuple-element.34), kind=kCustom, calls=%fused_computation.15 | custom fusion | bytes 4719104 | tf_op jit(solution)/shard_map/vmap()/gather | solution.py:41
  237.0 17.0 %gather_fusion.8 = bf16[32,2,144,128]{2,1,3,0:T(2,128)(2,1)} fusion(bf16[32,2,144,384]{2,1,0,3:T(2,128)(2,1)} %copy.58, s32[32]{0:T(128)S(1)} %get-tuple-element.35), kind=kCustom, calls=%fused_computation.16 | custom fusion | bytes 4719104 | tf_op jit(solution)/shard_map/vmap()/gather | solution.py:42
  254.1 9.3 %copy.44 = bf16[32,2,144,128]{3,2,1,0:T(8,128)(2,1)S(1)} copy(bf16[32,2,144,128]{2,1,3,0:T(2,128)(2,1)} %gather_fusion.5) | data formatting | bytes 4718592 | tf_op jit(solution)/shard_map/vmap()/gather | solution.py:41
  263.4 10.6 %copy.46 = bf16[32,2,144,128]{3,2,1,0:T(8,128)(2,1)} copy(bf16[32,2,144,128]{2,1,3,0:T(2,128)(2,1)} %gather_fusion.6) | data formatting | bytes 4718592 | tf_op jit(solution)/shard_map/vmap()/gather | solution.py:42
  274.0 10.7 %copy.59 = bf16[32,2,144,128]{3,2,1,0:T(8,128)(2,1)} copy(bf16[32,2,144,128]{2,1,3,0:T(2,128)(2,1)} %gather_fusion.7) | data formatting | bytes 4718592 | tf_op jit(solution)/shard_map/vmap()/gather | solution.py:41
  284.7 10.6 %copy.61 = bf16[32,2,144,128]{3,2,1,0:T(8,128)(2,1)} copy(bf16[32,2,144,128]{2,1,3,0:T(2,128)(2,1)} %gather_fusion.8) | data formatting | bytes 4718592 | tf_op jit(solution)/shard_map/vmap()/gather | solution.py:42
  295.3 6.6 %fusion.6 = (bf16[32,2,144,128,1]{3,2,1,0,4:T(8,128)(2,1)}, bf16[32,2,144,128,1]{3,2,1,0,4:T(8,128)(2,1)S(1)}) fusion(bf16[32,2,144,128]{3,2,1,0:T(8,128)(2,1)} %copy.46, bf16[32,2,144,128]{3,2,1,0:T(8,128)(2,1)S(1)} %copy.44, f32[32]{0:T(128)S(1)} %gather_fusion.3, f32[32]{0:T(128)S(1)} %gather_fusion, bf16[32,2,144,128]{3,2,1,0:T(8,128)(2,1)} %copy.61, ...), kind=kLoop, calls=%fused_computation.26 | loop fusion | flops 14155776 | bytes 14156032 | tf_op jit(solution)/shard_map/vmap()/convert_element_type | solution.py:46
  301.9 5.8 %fusion.15 = f32[4,2,144,128]{3,2,0,1:T(8,128)S(1)} fusion(bf16[32,4,144,144]{3,2,1,0:T(8,128)(2,1)} %reshape.126, bf16[32,2,144,128,1]{3,2,1,0,4:T(8,128)(2,1)S(1)} %get-tuple-element.31), kind=kOutput, calls=%fused_computation.31 | convolution fusion | flops 1358954496 | bytes 8257536 | tf_op jit(solution)/shard_map/qjmn,qrnc->jrmc/dot_general | solution.py:51
  307.7 0.1 copy.64
  307.9 0.2 copy.65
  308.0 0.1 copy.66
  308.2 0.2 copy.67
  308.3 0.1 copy.68
  308.5 0.2 copy.69
  308.6 0.1 copy.70
  308.8 0.2 copy.71
  308.9 6.6 %fusion.10 = f32[4,2,144,128]{3,2,0,1:T(8,128)S(1)} fusion(bf16[32,4,144,144]{3,2,1,0:T(8,128)(2,1)} %reshape.126, bf16[32,2,144,128,1]{3,2,1,0,4:T(8,128)(2,1)} %get-tuple-element.30), kind=kOutput, calls=%fused_computation.30 | convolution fusion | flops 1358954496 | bytes 8257536 | tf_op jit(solution)/shard_map/qjmn,qrnc->jrmc/dot_general | solution.py:51
  315.6 0.1 copy.49
  315.7 0.2 copy.50
  315.9 0.6 gather_fusion.13
  316.5 0.6 gather_fusion.9
  317.0 0.1 copy.51
  317.2 0.2 copy.52
  317.3 0.6 gather_fusion.14
  317.9 0.6 gather_fusion.10
  318.5 0.1 copy.53
  318.6 0.2 copy.54
  318.8 0.6 gather_fusion.15
  319.4 0.6 gather_fusion.11
  319.9 0.1 copy.55
  320.1 0.2 copy.56
  320.2 0.0 copy-start.1
  320.2 0.6 gather_fusion.16
  320.8 0.6 gather_fusion.12
  321.4 0.2 bitcast_add_fusion.3
  321.6 0.2 copy.57
  321.8 0.2 copy.72
  322.0 0.9 copy.73
  322.9 0.0 copy-done.1
  (13 shorter events, 0.2 us)
Async XLA Ops:
  0.0 73.9 %copy-start = (s32[32,32]{1,0:T(8,128)S(1)}, s32[32,32]{1,0:T(8,128)}, u32[]{:S(2)}) copy-start(s32[32,32]{1,0:T(8,128)} %param.11) | copy-start | bytes 12292
  0.0 53.1 %copy-start.2 = (s32[32]{0:T(128)S(1)}, s32[32]{0:T(128)}, u32[]{:S(2)}) copy-start(s32[32]{0:T(128)} %param.12) | copy-start | bytes 388
  0.0 53.9 %copy-start.3 = (f32[32]{0:T(128)S(1)}, f32[32]{0:T(128)}, u32[]{:S(2)}) copy-start(f32[32]{0:T(128)} %param.14) | copy-start | bytes 388
  0.0 54.6 %copy-start.4 = (f32[32]{0:T(128)S(1)}, f32[32]{0:T(128)}, u32[]{:S(2)}) copy-start(f32[32]{0:T(128)} %param.13) | copy-start | bytes 388
  39.0 63.8 %collective-permute-start = (bf16[32,2,144,128]{3,2,1,0:T(8,128)(2,1)S(1)}, bf16[32,2,144,128]{3,2,1,0:T(8,128)(2,1)}, u32[]{:S(2)}, u32[]{:S(2)}) collective-permute-start(bf16[32,2,144,128]{3,2,1,0:T(8,128)(2,1)S(1)} %bitcast.91), channel_id=1, source_target_pairs={{0,1},{1,2},{2,3},{3,4},{4,5},{5,6},{6,7},{7,8},{8,9},{9,10},{10,1... | collective-permute-start | bytes 7077896 | tf_op jit(solution)/shard_map/ppermute | solution.py:16
  42.8 61.1 %collective-permute-start.1 = (bf16[32,2,144,128]{3,2,1,0:T(8,128)(2,1)S(1)}, bf16[32,2,144,128]{3,2,1,0:T(8,128)(2,1)}, u32[]{:S(2)}, u32[]{:S(2)}) collective-permute-start(bf16[32,2,144,128]{3,2,1,0:T(8,128)(2,1)S(1)} %bitcast.92), channel_id=1, source_target_pairs={{1,0},{2,1},{3,2},{4,3},{5,4},{6,5},{7,6},{8,7},{9,8},{10,9},{11,1... | collective-permute-start | bytes 7077896 | tf_op jit(solution)/shard_map/ppermute | solution.py:17
  55.3 18.6 %copy-start.5 = (s32[16,4]{0,1:T(4,128)S(1)}, s32[16,4]{0,1:T(4,128)}, u32[]{:S(2)}) copy-start(s32[16,4]{0,1:T(4,128)} %param.15) | copy-start | bytes 772
  320.2 2.7 copy-start.1
